TPU v7x, 32 devices: a whole 2x2x4 slice. The times are simulated.
32 devices in a mesh: dp: 8 (over y, x, core), fsdp: 4 (over z).
Axes of the slice: x: 2, y: 2, z: 4, core: 2. Of those that a mesh axis runs over, the one named last changes fastest.
Arguments:
- tokens: bfloat16 [4096, 1152], P(('dp', 'fsdp')), may hold values from -6 to 6
- cotangent: bfloat16 [4096, 1152], P(('dp', 'fsdp')), may hold values from -6 to 6
- seq_ids: int32 [4096], P(('dp', 'fsdp')), may hold values from -1 to 127, as said below
- w_query: bfloat16 [1152, 1024], P(('dp', 'fsdp')), may hold values from -0.1875 to 0.1875
- w_key: bfloat16 [1152, 256], P(('dp', 'fsdp')), may hold values from -0.1875 to 0.1875
- w_value: bfloat16 [1152, 256], P(('dp', 'fsdp')), may hold values from -0.1875 to 0.1875
- w_output: bfloat16 [1024, 1152], P(('dp', 'fsdp')), may hold values from -0.1875 to 0.1875
- ffn_rows: bfloat16 [6912, 3456], P(('dp', 'fsdp')), may hold values from -0.1875 to 0.1875
- gain_attn_pre: bfloat16 [1152], P(('dp', 'fsdp')), may hold values from 0.099609375 to 1.8984375
- gain_attn_post: bfloat16 [1152], P(('dp', 'fsdp')), may hold values from 0.099609375 to 1.8984375
- gain_query: bfloat16 [256], P(('dp', 'fsdp')), may hold values from 0.099609375 to 1.8984375
- gain_key: bfloat16 [256], P(('dp', 'fsdp')), may hold values from 0.099609375 to 1.8984375
- gain_ffn_pre: bfloat16 [1152], P(('dp', 'fsdp')), may hold values from 0.099609375 to 1.8984375
- gain_ffn_post: bfloat16 [1152], P(('dp', 'fsdp')), may hold values from 0.099609375 to 1.8984375
Outputs:
- activations: bfloat16 [4096, 1152], P(('dp', 'fsdp'))
- token_grad: float32 [4096, 1152], P(('dp', 'fsdp'))
- grad_query: float32 [1152, 1024], P(('dp', 'fsdp'))
- grad_key: float32 [1152, 256], P(('dp', 'fsdp'))
- grad_value: float32 [1152, 256], P(('dp', 'fsdp'))
- grad_output: float32 [1024, 1152], P(('dp', 'fsdp'))
- grad_ffn_rows: float32 [6912, 3456], P(('dp', 'fsdp'))
- grad_attn_pre: float32 [1152], P(('dp', 'fsdp'))
- grad_attn_post: float32 [1152], P(('dp', 'fsdp'))
- grad_query_gain: float32 [256], P(('dp', 'fsdp'))
- grad_key_gain: float32 [256], P(('dp', 'fsdp'))
- grad_ffn_pre: float32 [1152], P(('dp', 'fsdp'))
- grad_ffn_post: float32 [1152], P(('dp', 'fsdp'))
Inputs may be any that keep to these rules, and one draw needn't show every extreme that they name: `seq_ids`: in each block of 128 rows the used slots come first and carry sequence numbers 0, 1, 2, ... in order; the rest are -1. A sequence has at most 96 rows and some sequence has exactly 96; every block has 96 or more used slots, some block is full, and some block holds 128 sequences of one row.
All inputs are finite; a program needn't handle non-finite values.
Results may differ from a plain program's by a relative error of at most 0.015.
Values may be sent and summed in bfloat16 or wider, within the bound.
No kernel may reach another device: no remote copies, remote signals or barrier semaphores. Data moves between devices by JAX's collectives and lax.ppermute only.
A program may use at most 448 MiB of HBM per device.

v0:
```python
import jax
import jax.numpy as jnp
from jax import lax
from jax.sharding import PartitionSpec as P

EPS = 1e-06
SCALE = 0.0625
BASE = 10000.0
CUBIC = 0.044715
ROOT_TERM = 0.7978845608028654


def normalize(values):
    factor = lax.rsqrt(jnp.mean(values * values, axis=-1, keepdims=True) + EPS)
    return (values * factor, factor)


def norm_back(incoming, unit, factor):
    return factor * (incoming - unit * jnp.mean(incoming * unit, axis=-1, keepdims=True))


def gelu_pair(values):
    tangent = jnp.tanh(ROOT_TERM * (values + CUBIC * values * values * values))
    result = 0.5 * values * (1.0 + tangent)
    slope = 0.5 * (1.0 + tangent) + 0.5 * values * (1.0 - tangent * tangent) * ROOT_TERM * (
        1.0 + 3.0 * CUBIC * values * values
    )
    return (result, slope)


def rotary(values, position, direction):
    half = values.shape[-1] // 2
    ladder = jnp.arange(half, dtype=jnp.float32) * (2.0 / values.shape[-1])
    freq = jnp.power(jnp.float32(BASE), -ladder)
    angle = position.astype(jnp.float32)[:, None] * freq[None, :]
    cosine = jnp.cos(angle)[:, None, :]
    sine = direction * jnp.sin(angle)[:, None, :]
    first = values[..., :half]
    second = values[..., half:]
    return jnp.concatenate(
        [first * cosine - second * sine, second * cosine + first * sine], axis=-1
    )


def layout_of(labels):
    count = labels.shape[0]
    index = jnp.arange(count, dtype=jnp.int32)
    same = labels[:, None] == labels[None, :]
    earlier = index[None, :] < index[:, None]
    position = jnp.sum(jnp.where(same & earlier, 1, 0), axis=1).astype(jnp.int32)
    allowed = same & (index[None, :] <= index[:, None])
    return (position, allowed)


def product(left, right):
    return jnp.dot(left, right, preferred_element_type=jnp.float32)


def cross_rows(left, right):
    return lax.dot_general(
        left, right, (((0,), (0,)), ((), ())), preferred_element_type=jnp.float32
    )


def cross_cols(left, right):
    return lax.dot_general(
        left, right, (((1,), (1,)), ((), ())), preferred_element_type=jnp.float32
    )


def batched(form, left, right):
    return jnp.einsum(form, left, right, preferred_element_type=jnp.float32)


def unpack(gathered):
    gains = tuple((item.astype(jnp.float32) for item in gathered[4:]))
    return (gathered[0], gathered[1], gathered[2], gathered[3], gains)


def attention_forward(attn_in, query_full, key_full, value_full, gain_q, gain_k, position, allowed):
    count = attn_in.shape[0]
    head_size = key_full.shape[1]
    heads = query_full.shape[1] // head_size
    queries = product(attn_in, query_full).reshape(count, heads, head_size)
    key_rows = product(attn_in, key_full)[:, None, :]
    value_rows = product(attn_in, value_full).astype(jnp.bfloat16)
    unit_query, factor_query = normalize(queries)
    unit_key, factor_key = normalize(key_rows)
    query_rot = rotary(unit_query * gain_q, position, 1.0).astype(jnp.bfloat16)
    key_rot = rotary(unit_key * gain_k, position, 1.0)[:, 0, :].astype(jnp.bfloat16)
    scores = batched("qhd,kd->hqk", query_rot, key_rot) * SCALE
    expo = jnp.where(allowed[None], jnp.exp(scores), 0.0)
    denom = jnp.sum(expo, axis=-1, keepdims=True)
    logsum = jnp.log(denom)
    probs = (expo / denom).astype(jnp.bfloat16)
    mixed = (
        batched("hqk,kd->qhd", probs, value_rows)
        .reshape(count, heads * head_size)
        .astype(jnp.bfloat16)
    )
    return (
        mixed,
        (unit_query, factor_query, unit_key, factor_key, query_rot, key_rot, value_rows, logsum),
    )


def attention_backward(d_mixed, saved, gain_q, gain_k, position, allowed):
    unit_query, factor_query, unit_key, factor_key, query_rot, key_rot, value_rows, logsum = saved
    count, heads, head_size = unit_query.shape
    d_heads = d_mixed.reshape(count, heads, head_size)
    scores = batched("qhd,kd->hqk", query_rot, key_rot) * SCALE
    probs_back = jnp.where(allowed[None], jnp.exp(scores - logsum), 0.0)
    d_probs = batched("qhd,kd->hqk", d_heads, value_rows)
    row_dot = jnp.sum(probs_back * d_probs, axis=-1, keepdims=True)
    d_scores = (probs_back * (d_probs - row_dot) * SCALE).astype(jnp.bfloat16)
    d_values = batched("hqk,qhd->kd", probs_back.astype(jnp.bfloat16), d_heads).astype(jnp.bfloat16)
    d_query_rot = batched("hqk,kd->qhd", d_scores, key_rot)
    d_key_rot = batched("hqk,qhd->kd", d_scores, query_rot)
    d_unit_query = rotary(d_query_rot, position, -1.0)
    d_unit_key = rotary(d_key_rot[:, None, :], position, -1.0)
    grad_qgain = jnp.sum(d_unit_query * unit_query, axis=(0, 1))
    grad_kgain = jnp.sum(d_unit_key * unit_key, axis=(0, 1))
    d_queries = (
        norm_back(d_unit_query * gain_q, unit_query, factor_query)
        .reshape(count, heads * head_size)
        .astype(jnp.bfloat16)
    )
    d_keys = norm_back(d_unit_key * gain_k, unit_key, factor_key)[:, 0, :].astype(jnp.bfloat16)
    return (d_queries, d_keys, d_values, grad_qgain, grad_kgain)


def local(
    tokens,
    cotangent,
    seq_ids,
    w_query,
    w_key,
    w_value,
    w_output,
    ffn_rows,
    gain_attn_pre,
    gain_attn_post,
    gain_query,
    gain_key,
    gain_ffn_pre,
    gain_ffn_post,
):
    count, width = tokens.shape
    shards = (
        w_query,
        w_key,
        w_value,
        w_output,
        gain_attn_pre,
        gain_attn_post,
        gain_query,
        gain_key,
        gain_ffn_pre,
        gain_ffn_post,
    )
    gathered = (
        lax.all_gather(shards[0], ("dp", "fsdp"), axis=0, tiled=True),
        lax.all_gather(shards[1], ("dp", "fsdp"), axis=0, tiled=True),
        lax.all_gather(shards[2], ("dp", "fsdp"), axis=0, tiled=True),
        lax.all_gather(shards[3], ("dp", "fsdp"), axis=0, tiled=True),
        lax.all_gather(shards[4], ("dp", "fsdp"), axis=0, tiled=True),
        lax.all_gather(shards[5], ("dp", "fsdp"), axis=0, tiled=True),
        lax.all_gather(shards[6], ("dp", "fsdp"), axis=0, tiled=True),
        lax.all_gather(shards[7], ("dp", "fsdp"), axis=0, tiled=True),
        lax.all_gather(shards[8], ("dp", "fsdp"), axis=0, tiled=True),
        lax.all_gather(shards[9], ("dp", "fsdp"), axis=0, tiled=True),
    )
    query_full, key_full, value_full, output_full, gains = unpack(gathered)
    g_attn_pre, g_attn_post, g_query, g_key, g_ffn_pre, g_ffn_post = gains
    position, allowed = layout_of(seq_ids)
    live = (seq_ids >= 0).astype(jnp.float32)[:, None]
    inputs = tokens.astype(jnp.float32)
    unit_in, factor_in = normalize(inputs)
    attn_in = (unit_in * g_attn_pre).astype(jnp.bfloat16)
    mixed, saved = attention_forward(
        attn_in, query_full, key_full, value_full, g_query, g_key, position, allowed
    )
    attn_raw = product(mixed, output_full)
    unit_post, factor_post = normalize(attn_raw)
    resid = inputs + unit_post * g_attn_post
    unit_ffn, factor_ffn = normalize(resid)
    ffn_in = (unit_ffn * g_ffn_pre).astype(jnp.bfloat16)
    piece = lax.all_gather(ffn_rows[:, : 2 * width], ("dp", "fsdp"), axis=0, tiled=True)
    gate_up = jnp.stack(
        [cross_cols(ffn_in, piece[:, :width]), cross_cols(ffn_in, piece[:, width:])], axis=0
    )
    gate_all = gate_up[0]
    up_all = gate_up[1]
    gelu_all, slope_all = gelu_pair(gate_all)
    hidden_all = (gelu_all * up_all).astype(jnp.bfloat16)
    ffn_raw = product(
        hidden_all, lax.all_gather(ffn_rows[:, 2 * width :], ("dp", "fsdp"), axis=0, tiled=True)
    )
    unit_last, factor_last = normalize(ffn_raw)
    out_rows = resid + unit_last * g_ffn_post
    activations = (live * out_rows).astype(jnp.bfloat16)
    back_weights = (
        lax.all_gather(shards[0], ("dp", "fsdp"), axis=0, tiled=True),
        lax.all_gather(shards[1], ("dp", "fsdp"), axis=0, tiled=True),
        lax.all_gather(shards[2], ("dp", "fsdp"), axis=0, tiled=True),
        lax.all_gather(shards[3], ("dp", "fsdp"), axis=0, tiled=True),
        lax.all_gather(shards[4], ("dp", "fsdp"), axis=0, tiled=True),
        lax.all_gather(shards[5], ("dp", "fsdp"), axis=0, tiled=True),
        lax.all_gather(shards[6], ("dp", "fsdp"), axis=0, tiled=True),
        lax.all_gather(shards[7], ("dp", "fsdp"), axis=0, tiled=True),
        lax.all_gather(shards[8], ("dp", "fsdp"), axis=0, tiled=True),
        lax.all_gather(shards[9], ("dp", "fsdp"), axis=0, tiled=True),
    )
    query_back, key_back, value_back, output_back, back_gains = unpack(back_weights)
    b_attn_pre, b_attn_post, b_query, b_key, b_ffn_pre, b_ffn_post = back_gains
    cot_live = cotangent.astype(jnp.float32) * live
    grad_ffn_post = jnp.sum(cot_live * unit_last, axis=0)
    d_ffn_raw = norm_back(cot_live * b_ffn_post, unit_last, factor_last).astype(jnp.bfloat16)
    piece = lax.all_gather(ffn_rows, ("dp", "fsdp"), axis=0, tiled=True)
    up_rows = up_all
    gelu_val = gelu_all
    gelu_slope = slope_all
    d_hidden = cross_cols(d_ffn_raw, piece[:, 2 * width :])
    d_gate = (d_hidden * up_rows * gelu_slope).astype(jnp.bfloat16)
    d_up = (d_hidden * gelu_val).astype(jnp.bfloat16)
    d_ffn_in = product(d_gate, piece[:, :width]) + product(d_up, piece[:, width : 2 * width])
    local_gate = ffn_rows[:, :width]
    local_up = ffn_rows[:, width : 2 * width]
    local_down = ffn_rows[:, 2 * width :]
    rows_in = lax.all_gather(ffn_in, ("dp", "fsdp"), axis=0, tiled=True)
    rows_back = lax.all_gather(d_ffn_raw, ("dp", "fsdp"), axis=0, tiled=True)
    gate = cross_cols(rows_in, local_gate)
    up_rows = cross_cols(rows_in, local_up)
    gelu_val, gelu_slope = gelu_pair(gate)
    hidden = (gelu_val * up_rows).astype(jnp.bfloat16)
    d_hidden = cross_cols(rows_back, local_down)
    d_gate = (d_hidden * up_rows * gelu_slope).astype(jnp.bfloat16)
    d_up = (d_hidden * gelu_val).astype(jnp.bfloat16)
    grad_ffn = jnp.concatenate(
        [cross_rows(d_gate, rows_in), cross_rows(d_up, rows_in), cross_rows(hidden, rows_back)],
        axis=1,
    )
    grad_ffn_pre = jnp.sum(d_ffn_in * unit_ffn, axis=0)
    d_resid = cot_live + norm_back(d_ffn_in * b_ffn_pre, unit_ffn, factor_ffn)
    grad_attn_post = jnp.sum(d_resid * unit_post, axis=0)
    d_attn_raw = norm_back(d_resid * b_attn_post, unit_post, factor_post).astype(jnp.bfloat16)
    grad_output = cross_rows(mixed, d_attn_raw)
    d_mixed = cross_cols(d_attn_raw, output_back).astype(jnp.bfloat16)
    d_queries, d_keys, d_values, grad_qgain, grad_kgain = attention_backward(
        d_mixed, saved, b_query, b_key, position, allowed
    )
    grad_query = cross_rows(attn_in, d_queries)
    grad_key = cross_rows(attn_in, d_keys)
    grad_value = cross_rows(attn_in, d_values)
    d_attn_in = (
        cross_cols(d_queries, query_back)
        + cross_cols(d_keys, key_back)
        + cross_cols(d_values, value_back)
    )
    grad_attn_pre = jnp.sum(d_attn_in * unit_in, axis=0)
    token_grad = d_resid + norm_back(d_attn_in * b_attn_pre, unit_in, factor_in)
    summed = (
        lax.psum_scatter(grad_query, ("dp", "fsdp"), scatter_dimension=0, tiled=True),
        lax.psum_scatter(grad_key, ("dp", "fsdp"), scatter_dimension=0, tiled=True),
        lax.psum_scatter(grad_value, ("dp", "fsdp"), scatter_dimension=0, tiled=True),
        lax.psum_scatter(grad_output, ("dp", "fsdp"), scatter_dimension=0, tiled=True),
        lax.psum_scatter(grad_attn_pre, ("dp", "fsdp"), scatter_dimension=0, tiled=True),
        lax.psum_scatter(grad_attn_post, ("dp", "fsdp"), scatter_dimension=0, tiled=True),
        lax.psum_scatter(grad_qgain, ("dp", "fsdp"), scatter_dimension=0, tiled=True),
        lax.psum_scatter(grad_kgain, ("dp", "fsdp"), scatter_dimension=0, tiled=True),
        lax.psum_scatter(grad_ffn_pre, ("dp", "fsdp"), scatter_dimension=0, tiled=True),
        lax.psum_scatter(grad_ffn_post, ("dp", "fsdp"), scatter_dimension=0, tiled=True),
    )
    return (
        activations,
        token_grad,
        summed[0],
        summed[1],
        summed[2],
        summed[3],
        grad_ffn,
        summed[4],
        summed[5],
        summed[6],
        summed[7],
        summed[8],
        summed[9],
    )


def solution(mesh):
    return jax.shard_map(
        local,
        mesh=mesh,
        in_specs=(
            P(("dp", "fsdp"), None),
            P(("dp", "fsdp"), None),
            P(("dp", "fsdp")),
            P(("dp", "fsdp"), None),
            P(("dp", "fsdp"), None),
            P(("dp", "fsdp"), None),
            P(("dp", "fsdp"), None),
            P(("dp", "fsdp"), None),
            P(("dp", "fsdp")),
            P(("dp", "fsdp")),
            P(("dp", "fsdp")),
            P(("dp", "fsdp")),
            P(("dp", "fsdp")),
            P(("dp", "fsdp")),
        ),
        out_specs=(
            P(("dp", "fsdp"), None),
            P(("dp", "fsdp"), None),
            P(("dp", "fsdp"), None),
            P(("dp", "fsdp"), None),
            P(("dp", "fsdp"), None),
            P(("dp", "fsdp"), None),
            P(("dp", "fsdp"), None),
            P(("dp", "fsdp")),
            P(("dp", "fsdp")),
            P(("dp", "fsdp")),
            P(("dp", "fsdp")),
            P(("dp", "fsdp")),
            P(("dp", "fsdp")),
        ),
        check_vma=False,
    )
```

profile of v0, /device:TPU:4, one launch (start us, length us, event | category | flops | bytes accessed | tf_op | source)
XLA Modules:
  0.0 1220.8 jit_solution(15145468353143789515)
XLA Ops:
  14.6 42.4 %all-reduce.19 = (bf16[1152]{0:T(1024)(128)(2,1)S(1)}, bf16[256]{0:T(256)(128)(2,1)S(1)}, bf16[256]{0:T(256)(128)(2,1)S(1)}, bf16[1152]{0:T(1024)(128)(2,1)S(1)}...) all-reduce(bf16[1152]{0:T(1024)(128)(2,1)S(1)} %dynamic-update-slic, ...), channel_id=1, replica_groups=mesh['dp'=8,'fsdp'=4] {'dp','fsdp'}, use_global_device_ids=true, to_apply=%add | all-reduce | flops 5120 | bytes 20480
  57.0 72.8 %all-gather = bf16[32,36,256]{2,1,0:T(8,128)(2,1)S(1)} all-gather(bf16[1,36,256]{2,1,0:T(8,128)(2,1)S(1)} %bitcast.102), channel_id=1, replica_groups=mesh['dp'=8,'fsdp'=4] {'dp','fsdp'}, dimensions={0}, use_global_device_ids=true | all-gather | bytes 608256 | tf_op jit(solution)/shard_map/all_gather | solution.py:164
  130.2 77.4 %all-gather.1 = bf16[32,36,256]{2,1,0:T(8,128)(2,1)S(1)} all-gather(bf16[1,36,256]{2,1,0:T(8,128)(2,1)S(1)} %bitcast.103), channel_id=1, replica_groups=mesh['dp'=8,'fsdp'=4] {'dp','fsdp'}, dimensions={0}, use_global_device_ids=true | all-gather | bytes 608256 | tf_op jit(solution)/shard_map/all_gather | solution.py:163
  211.3 2.7 reshape.363
  226.1 98.5 %all-gather.13.cloned.1.call-done = bf16[6912,2304]{1,0:T(8,128)(2,1)} async-done(((bf16[216,2304]{1,0:T(8,128)(2,1)}), bf16[6912,2304]{1,0:T(8,128)(2,1)}) %all-gather.13.cloned.1.call-update) | async-done | bytes 31850512 | tf_op jit(solution)/shard_map/all_gather | solution.py:188
  324.6 11.9 fusion.10
  336.4 11.7 fusion.12
  348.1 88.0 %all-gather.15.cloned.1.call-done = bf16[6912,1152]{1,0:T(8,128)(2,1)} async-done(((bf16[216,1152]{1,0:T(8,128)(2,1)}), bf16[6912,1152]{1,0:T(8,128)(2,1)}) %all-gather.15.cloned.1.call-update) | async-done | bytes 15925264 | tf_op jit(solution)/shard_map/all_gather | solution.py:197
  436.1 10.7 multiply_reduce_fusion.6
  455.7 62.9 %all-gather.21.cloned.1.call-done = bf16[4096,1152]{1,0:T(8,128)(2,1)} async-done(((bf16[128,1152]{1,0:T(8,128)(2,1)}), bf16[4096,1152]{1,0:T(8,128)(2,1)}) %all-gather.21.cloned.1.call-update) | async-done | bytes 9437200 | tf_op jit(solution)/shard_map/all_gather | solution.py:230
  518.5 8.9 fusion.63
  527.5 6.1 fusion.61
  533.5 67.7 %all-gather.19.cloned.1.call-done = bf16[4096,1152]{1,0:T(8,128)(2,1)} async-done(((bf16[128,1152]{1,0:T(8,128)(2,1)}), bf16[4096,1152]{1,0:T(8,128)(2,1)}) %all-gather.19.cloned.1.call-update) | async-done | bytes 9437200 | tf_op jit(solution)/shard_map/all_gather | solution.py:231
  601.2 9.1 fusion.136
  610.3 7.0 fusion.33
  617.4 5.1 fusion.32
  622.5 4.2 fusion.40
  628.4 236.6 %all-gather.17.cloned.1.call-done = bf16[6912,3456]{1,0:T(8,128)(2,1)} async-done(((bf16[216,3456]{1,0:T(8,128)(2,1)}), bf16[6912,3456]{1,0:T(8,128)(2,1)}) %all-gather.17.cloned.1.call-update) | async-done | bytes 47775760 | tf_op jit(solution)/shard_map/all_gather | solution.py:219
  865.1 11.8 fusion.8
  876.8 10.7 fusion.4
  887.7 10.1 multiply_reduce_fusion.1
  899.6 2.9 fusion.151
  902.6 2.6 convolution_convert_fusion
  921.5 3.1 fusion.142
  924.5 194.9 %fusion.149 = (f32[40,1024]{1,0:T(8,128)S(1)}, f32[40,256]{1,0:T(8,128)S(1)}, f32[40,256]{1,0:T(8,128)S(1)}) fusion(f32[1152,1024]{1,0:T(8,128)} %fusion.142, f32[1152,256]{1,0:T(8,128)} %fusion.140, f32[1152,256]{1,0:T(8,128)} %fusion.138), kind=kCustom, calls=%all-reduce-scatter.3 | all-reduce-scatter fusion | flops 1966081 | bytes 7323648
  1129.7 4.8 collective-permute-start.10
  1137.6 42.0 %all-reduce.18 = (f32[1152]{0:T(1024)S(1)}, f32[1152]{0:T(1024)S(1)}, f32[256]{0:T(256)S(1)}, f32[256]{0:T(256)S(1)}, f32[1152]{0:T(1024)S(1)}, /*index=5*/f32[1152]{0:T(1024)S(1)}) all-reduce(f32[1152]{0:T(1024)S(1)} %get-tuple-element.19, f32[1152]{0:T(1024)S(1)} %copy-done.32, ...), channel_id=6, replica_groups=mesh['dp'=8,'fsdp'=4] {'dp','fsdp'}, use_global_device_ids=true, to_apply=%region_20.21.clone | all-reduce | flops 5120 | bytes 40960
  1183.0 4.2 collective-permute-start.2
  1192.2 3.3 collective-permute-start.9
  1195.5 4.7 collective-permute-start.8
  1200.8 5.4 collective-permute-done.9
  1209.3 2.8 collective-permute-done.3
  (306 shorter events, 78.2 us)
Async XLA Ops:
  7.2 49.8 %copy-start.37 = (bf16[36,256]{1,0:T(8,128)(2,1)S(1)}, bf16[36,256]{1,0:T(8,128)(2,1)}, u32[]{:S(2)}) copy-start(bf16[36,256]{1,0:T(8,128)(2,1)} %param.19) | copy-start | bytes 55300
  7.3 122.8 %copy-start.62 = (s32[128]{0:T(128)S(1)}, s32[128]{0:T(128)}, u32[]{:S(2)}) copy-start(s32[128]{0:T(128)} %param.16) | copy-start | bytes 1540
  7.3 122.9 %copy-start.38 = (bf16[36,256]{1,0:T(8,128)(2,1)S(1)}, bf16[36,256]{1,0:T(8,128)(2,1)}, u32[]{:S(2)}) copy-start(bf16[36,256]{1,0:T(8,128)(2,1)} %param.18) | copy-start | bytes 55300
  7.3 204.0 %all-gather.23.cloned.1.call-start = ((), (), s32[]{:S(2)}) async-start(), calls=%async_computation.8 | async-start | bytes 2703360 | tf_op jit(solution)/shard_map/all_gather | solution.py:162
  8.0 211.3 %all-gather.11.cloned.1.call-start = ((), (), s32[]{:S(2)}) async-start(), calls=%async_computation.1 | async-start | bytes 2433024 | tf_op jit(solution)/shard_map/all_gather | solution.py:165
  8.8 315.8 %all-gather.13.cloned.1.call-start = ((), (), s32[]{:S(2)}) async-start(), calls=%async_computation.2 | async-start | bytes 32845824 | tf_op jit(solution)/shard_map/all_gather | solution.py:188
  11.0 196.7 %copy-start = (bf16[128,1152]{1,0:T(8,128)(2,1)S(1)}, bf16[128,1152]{1,0:T(8,128)(2,1)}, u32[]{:S(2)}) copy-start(bf16[128,1152]{1,0:T(8,128)(2,1)} %param.14) | copy-start | bytes 884740
  11.1 425.1 %all-gather.15.cloned.1.call-start = ((), (), s32[]{:S(2)}) async-start(), calls=%async_computation.3 | async-start | bytes 16422912 | tf_op jit(solution)/shard_map/all_gather | solution.py:197
  13.0 505.5 %all-gather.21.cloned.1.call-start = ((), (), s32[]{:S(2)}) async-start(), calls=%async_computation.7 | async-start | bytes 9732096 | tf_op jit(solution)/shard_map/all_gather | solution.py:230
  130.0 81.3 %copy-start.11 = (bf16[1152,256]{1,0:T(8,128)(2,1)}, bf16[1152,256]{1,0:T(8,128)(2,1)S(1)}, u32[]{:S(2)}) copy-start(bf16[1152,256]{1,0:T(8,128)(2,1)S(1)} %reshape.359) | copy-start | bytes 1769476
  130.0 86.9 %copy-start.46 = (f32[256]{0:T(256)}, f32[256]{0:T(256)S(1)}, u32[]{:S(2)}) copy-start(f32[256]{0:T(256)S(1)} %convert_element_type.122) | copy-start | bytes 3076
  130.1 83.8 %copy-start.51 = (f32[128]{0:T(128)}, f32[128]{0:T(128)S(1)}, u32[]{:S(2)}) copy-start(f32[128]{0:T(128)S(1)} %convert_element_type.120) | copy-start | bytes 1540
  207.7 15.1 %copy-start.28 = (f32[1152]{0:T(1024)}, f32[1152]{0:T(1024)S(1)}, u32[]{:S(2)}) copy-start(f32[1152]{0:T(1024)S(1)} %convert_element_type.128) | copy-start | bytes 13828
  224.4 376.8 %all-gather.19.cloned.1.call-start = ((), (), s32[]{:S(2)}) async-start(), calls=%async_computation.6 | async-start | bytes 9732096 | tf_op jit(solution)/shard_map/all_gather | solution.py:231
  226.1 110.3 %copy-start.16 = (bf16[128,1152]{1,0:T(8,128)(2,1)S(1)}, bf16[128,1152]{1,0:T(8,128)(2,1)}, u32[]{:S(2)}) copy-start(bf16[128,1152]{1,0:T(8,128)(2,1)} %multiply_convert_fusion.11) | copy-start | bytes 884740
  348.1 98.7 %copy-start.8 = (bf16[128,1152]{1,0:T(8,128)(2,1)S(1)}, bf16[128,1152]{1,0:T(8,128)(2,1)}, u32[]{:S(2)}) copy-start(bf16[128,1152]{1,0:T(8,128)(2,1)} %param.15) | copy-start | bytes 884740
  448.8 416.2 %all-gather.17.cloned.1.call-start = ((), (), s32[]{:S(2)}) async-start(), calls=%async_computation.4 | async-start | bytes 49268736 | tf_op jit(solution)/shard_map/all_gather | solution.py:219
  449.6 764.0 %reduce-scatter.8.cloned.1.call-start = ((), (), s32[]{:S(2)}) async-start(), calls=%async_computation.5 | async-start | bytes 4866048 | tf_op jit(solution)/shard_map/reduce_scatter | solution.py:266
  601.2 16.1 %slice-start = ((s8[9437184]{0:T(1024)(128)(4,1)}), s8[4194304]{0:T(1024)(128)(4,1)S(1)}, s32[]{:S(2)}) async-start(s8[9437184]{0:T(1024)(128)(4,1)} %bitcast.105), calls=%async_computation.9 | async-start | bytes 8388608
  1119.5 16.9 %copy-start.7 = (f32[128,1152]{1,0:T(8,128)S(1)}, f32[128,1152]{1,0:T(8,128)}, u32[]{:S(2)}) copy-start(f32[128,1152]{1,0:T(8,128)} %copy-done.6) | copy-start | bytes 1769476
  1119.5 63.5 %collective-permute-start.6 = (f32[40,256]{1,0:T(8,128)S(1)}, f32[40,256]{1,0:T(8,128)S(1)}, u32[]{:S(2)}, u32[]{:S(2)}) collective-permute-start(f32[40,256]{1,0:T(8,128)S(1)} %get-tuple-element.39), channel_id=1, source_target_pairs={{0,3},{1,4},{2,5},{3,6},{4,7},{5,8},{6,9},{7,10},{8,11},{9,12},{10... | collective-permute-start | bytes 122888
  1121.6 65.6 %collective-permute-start.5 = (f32[40,256]{1,0:T(8,128)S(1)}, f32[40,256]{1,0:T(8,128)S(1)}, u32[]{:S(2)}, u32[]{:S(2)}) collective-permute-start(f32[40,256]{1,0:T(8,128)S(1)} %get-tuple-element.39), channel_id=1, source_target_pairs={{0,2},{1,3},{2,4},{3,5},{4,6},{5,7},{6,8},{7,9},{8,10},{9,11},{10,... | collective-permute-start | bytes 122888
  1123.5 65.7 %collective-permute-start.4 = (f32[40,256]{1,0:T(8,128)S(1)}, f32[40,256]{1,0:T(8,128)S(1)}, u32[]{:S(2)}, u32[]{:S(2)}) collective-permute-start(f32[40,256]{1,0:T(8,128)S(1)} %get-tuple-element.39), channel_id=1, source_target_pairs={{0,1},{1,2},{2,3},{3,4},{4,5},{5,6},{6,7},{7,8},{8,9},{9,10},{10,1... | collective-permute-start | bytes 122888
  1125.4 9.1 collective-permute-start.7
  1129.7 65.8 %collective-permute-start.10 = (f32[40,256]{1,0:T(8,128)S(1)}, f32[40,256]{1,0:T(8,128)S(1)}, u32[]{:S(2)}, u32[]{:S(2)}) collective-permute-start(f32[40,256]{1,0:T(8,128)S(1)} %get-tuple-element.40), channel_id=1, source_target_pairs={{0,3},{1,4},{2,5},{3,6},{4,7},{5,8},{6,9},{7,10},{8,11},{9,12},{10... | collective-permute-start | bytes 122888
  1134.5 57.7 %collective-permute-start.11 = (f32[4,256]{1,0:T(4,128)S(1)}, f32[4,256]{1,0:T(4,128)S(1)}, u32[]{:S(2)}, u32[]{:S(2)}) collective-permute-start(f32[4,256]{1,0:T(4,128)S(1)} %slice.84), channel_id=1, source_target_pairs={{0,4},{1,5},{2,6},{3,7},{4,8},{5,9},{6,10},{7,11},{8,12},{9,13},{1... | collective-permute-start | bytes 12296
  1183.0 29.1 %collective-permute-start.2 = (f32[40,1024]{1,0:T(8,128)S(1)}, f32[40,1024]{1,0:T(8,128)S(1)}, u32[]{:S(2)}, u32[]{:S(2)}) collective-permute-start(f32[40,1024]{1,0:T(8,128)S(1)} %get-tuple-element.38), channel_id=1, source_target_pairs={{0,3},{1,4},{2,5},{3,6},{4,7},{5,8},{6,9},{7,10},{8,11},{9,12},{10... | collective-permute-start | bytes 491528
  1187.2 25.0 %collective-permute-start.1 = (f32[40,1024]{1,0:T(8,128)S(1)}, f32[40,1024]{1,0:T(8,128)S(1)}, u32[]{:S(2)}, u32[]{:S(2)}) collective-permute-start(f32[40,1024]{1,0:T(8,128)S(1)} %get-tuple-element.38), channel_id=1, source_target_pairs={{0,2},{1,3},{2,4},{3,5},{4,6},{5,7},{6,8},{7,9},{8,10},{9,11},{10,... | collective-permute-start | bytes 491528
  1189.2 23.0 %collective-permute-start = (f32[40,1024]{1,0:T(8,128)S(1)}, f32[40,1024]{1,0:T(8,128)S(1)}, u32[]{:S(2)}, u32[]{:S(2)}) collective-permute-start(f32[40,1024]{1,0:T(8,128)S(1)} %get-tuple-element.38), channel_id=1, source_target_pairs={{0,1},{1,2},{2,3},{3,4},{4,5},{5,6},{6,7},{7,8},{8,9},{9,10},{10,1... | collective-permute-start | bytes 491528
  1192.2 14.0 %collective-permute-start.9 = (f32[40,256]{1,0:T(8,128)S(1)}, f32[40,256]{1,0:T(8,128)S(1)}, u32[]{:S(2)}, u32[]{:S(2)}) collective-permute-start(f32[40,256]{1,0:T(8,128)S(1)} %get-tuple-element.40), channel_id=1, source_target_pairs={{0,2},{1,3},{2,4},{3,5},{4,6},{5,7},{6,8},{7,9},{8,10},{9,11},{10,... | collective-permute-start | bytes 122888
  1195.5 12.7 %collective-permute-start.8 = (f32[40,256]{1,0:T(8,128)S(1)}, f32[40,256]{1,0:T(8,128)S(1)}, u32[]{:S(2)}, u32[]{:S(2)}) collective-permute-start(f32[40,256]{1,0:T(8,128)S(1)} %get-tuple-element.40), channel_id=1, source_target_pairs={{0,1},{1,2},{2,3},{3,4},{4,5},{5,6},{6,7},{7,8},{8,9},{9,10},{10,1... | collective-permute-start | bytes 122888
  1206.2 5.9 collective-permute-start.3
  (70 other events, 432.6 us)
Sparse Core Ops, SparseCore 0:
  10.9 59.1 all-gather.22
  72.9 56.4 all-gather.10
  132.8 191.6 all-gather.12
  327.3 108.8 all-gather.14
  438.8 79.7 all-gather.20
  521.2 79.9 all-gather.18
  604.1 260.9 all-gather.16
  911.6 118.7 reduce-scatter.7
where the time goes:
time: 1230 us; the launch traced here: 1220 us
  waiting for transfers between devices  564 us (46%)
  blocking collectives  430 us (35%)
  matrix products  133 us (11%)
  starting transfers between devices  34.5 us (3%)
  local copies, waits for them, and re-layouts  29.1 us (2%)
  between operations  15.9 us (1%)
  other arithmetic  15.1 us (1%)
    unnamed x3, blocking collectives  279 us
    all_gather x1, waiting for transfers between devices, local(): piece = lax.all_gather(ffn_rows, ('dp', 'fsdp'), axis=0, tiled=True)  237 us
    all_gather x1, waiting for transfers between devices, local(): lax.all_gather(ffn_rows[:, :2 * width], ('dp', 'fsdp'), axis=0, tiled=True)  98.5 us
    all_gather x1, waiting for transfers between devices, local(): lax.all_gather(ffn_rows[:, 2 * width:], ('dp', 'fsdp'), axis=0, tiled=True)  88 us
    all_gather x1, blocking collectives, local(): lax.all_gather(shards[1], ('dp', 'fsdp'), axis=0, tiled=True)  77.4 us
    all_gather x1, blocking collectives, local(): lax.all_gather(shards[2], ('dp', 'fsdp'), axis=0, tiled=True)  72.8 us
    all_gather x1, waiting for transfers between devices, local(): rows_back = lax.all_gather(d_ffn_raw, ('dp', 'fsdp'), axis=0, tiled=True)  67.7 us
    dot_general x10, matrix products, cross_cols(): lax.dot_general(left, right, (((1,), (1,)), ((), ())), preferred_element_...  63.6 us
  transfers between devices with their start and end apart: 20, of which 7 were waited for; matrix products, arithmetic and copies ran while one was open for 26% of the time, Pallas kernels for 0%

commit v1 on v0

v1 whole, which is shorter than its diff:
```python
import jax
import jax.numpy as jnp
from jax import lax
from jax.sharding import PartitionSpec as P

EPS = 1e-06
SCALE = 0.0625
BASE = 10000.0
CUBIC = 0.044715
ROOT_TERM = 0.7978845608028654
F32 = jnp.float32
BF16 = jnp.bfloat16


def normalize(values):
    factor = lax.rsqrt(jnp.mean(values * values, axis=-1, keepdims=True) + EPS)
    return (values * factor, factor)


def norm_back(incoming, unit, factor):
    return factor * (incoming - unit * jnp.mean(incoming * unit, axis=-1, keepdims=True))


def gelu_pair(values):
    tangent = jnp.tanh(ROOT_TERM * (values + CUBIC * values * values * values))
    result = 0.5 * values * (1.0 + tangent)
    slope = 0.5 * (1.0 + tangent) + 0.5 * values * (1.0 - tangent * tangent) * ROOT_TERM * (
        1.0 + 3.0 * CUBIC * values * values
    )
    return (result, slope)


def rotary_tables(position, size):
    half = size // 2
    ladder = jnp.arange(half, dtype=F32) * (2.0 / size)
    freq = jnp.power(jnp.float32(BASE), -ladder)
    angle = position.astype(F32)[:, None] * freq[None, :]
    return (jnp.cos(angle), jnp.sin(angle))


def rotary(values, cosine, sine):
    half = values.shape[-1] // 2
    first = values[..., :half]
    second = values[..., half:]
    cosine = cosine[:, None, :]
    sine = sine[:, None, :]
    return jnp.concatenate(
        [first * cosine - second * sine, second * cosine + first * sine], axis=-1
    )


def layout_of(labels):
    count = labels.shape[0]
    index = jnp.arange(count, dtype=jnp.int32)
    same = labels[:, None] == labels[None, :]
    earlier = index[None, :] < index[:, None]
    position = jnp.sum(jnp.where(same & earlier, 1, 0), axis=1).astype(jnp.int32)
    allowed = same & (index[None, :] <= index[:, None])
    return (position, allowed)


def product(left, right):
    return jnp.dot(left, right, preferred_element_type=F32)


def cross_rows(left, right):
    return lax.dot_general(left, right, (((0,), (0,)), ((), ())), preferred_element_type=F32)


def cross_cols(left, right):
    return lax.dot_general(left, right, (((1,), (1,)), ((), ())), preferred_element_type=F32)


def batched(form, left, right):
    return jnp.einsum(form, left, right, preferred_element_type=F32)


class Links:
    def __init__(self, mesh):
        self.dp = mesh.shape["dp"]
        self.fsdp = mesh.shape["fsdp"]
        assert self.dp & (self.dp - 1) == 0 and self.fsdp & (self.fsdp - 1) == 0
        count = self.dp.bit_length() - 1
        self.bits = [1] + [1 << i for i in range(count - 1, 0, -1)] if count else []
        self.wires = self.bits[1:]
        self.total = self.dp * self.fsdp

    def swap(self, value, axis, offset):
        size = self.dp if axis == "dp" else self.fsdp
        return lax.ppermute(value, axis, [(i, i ^ offset) for i in range(size)])

    def lift(self, value):
        return value.reshape((1,) * (len(self.bits) + 1) + value.shape)

    def gather_line(self, value):
        parts = [value] + [self.swap(value, "fsdp", k) for k in range(1, self.fsdp)]
        return jnp.concatenate(parts, axis=len(self.bits))

    def gather_bit(self, value, bit):
        return jnp.concatenate([value, self.swap(value, "dp", bit)], axis=self.bits.index(bit))

    def gather_plane(self, value, order):
        for bit in order:
            value = self.gather_bit(value, bit)
        return value

    def orders(self):
        return (self.wires, self.wires[::-1])

    def reduce_bit(self, value, bit):
        axis = self.bits.index(bit)
        keep = lax.slice_in_dim(value, 0, 1, axis=axis)
        send = lax.slice_in_dim(value, 1, 2, axis=axis).astype(BF16)
        return keep.astype(F32) + self.swap(send, "dp", bit).astype(F32)

    def reduce_line(self, value):
        axis = len(self.bits)
        total = lax.slice_in_dim(value, 0, 1, axis=axis).astype(F32)
        for k in range(1, self.fsdp):
            send = lax.slice_in_dim(value, k, k + 1, axis=axis).astype(BF16)
            total = total + self.swap(send, "fsdp", k).astype(F32)
        return total

    def owners(self):
        shape = (2,) * len(self.bits) + (self.fsdp,)
        index = jnp.arange(self.total, dtype=jnp.int32)
        line = index % self.fsdp
        rest = index // self.fsdp
        offset = jnp.zeros_like(index)
        for bit in self.bits[::-1]:
            offset = offset + (rest % 2) * bit
            rest = rest // 2
        return (lax.axis_index("dp") ^ offset) * self.fsdp + (lax.axis_index("fsdp") ^ line)


def one_hot_rows(owners, rows, padded):
    inner = jnp.arange(padded, dtype=jnp.int32)
    target = jnp.where(inner[None, :] < rows, owners[:, None] * rows + inner[None, :], -1)
    size = owners.shape[0] * rows
    return (jnp.arange(size, dtype=jnp.int32)[:, None] == target.reshape(-1)[None, :]).astype(BF16)


def split3(value):
    high = value.astype(BF16)
    rest = value - high.astype(F32)
    middle = rest.astype(BF16)
    low = (rest - middle.astype(F32)).astype(BF16)
    return (high, middle, low)


def make_local(mesh):
    links = Links(mesh)

    def local(
        tokens,
        cotangent,
        seq_ids,
        w_query,
        w_key,
        w_value,
        w_output,
        ffn_rows,
        gain_attn_pre,
        gain_attn_post,
        gain_query,
        gain_key,
        gain_ffn_pre,
        gain_ffn_post,
    ):
        count, width = tokens.shape
        rows = w_query.shape[0]
        q_width = w_query.shape[1]
        head_size = w_key.shape[1]
        heads = q_width // head_size
        out_rows_n = w_output.shape[0]
        padded = (rows + 8) // 8 * 8
        n = links.total
        small = gain_query.shape[0]

        packed = jnp.concatenate([w_query, w_key, w_value], axis=1)
        wide = packed.shape[1]
        gain_row = jnp.concatenate(
            [gain_attn_pre, gain_attn_post, gain_ffn_pre, gain_ffn_post, gain_query, gain_key]
        )
        gain_n = gain_row.shape[0]
        tail = jnp.pad(gain_row[None, :], ((0, padded - rows - 1), (0, wide - gain_n)))
        packed = jnp.concatenate([packed, tail], axis=0)
        half = wide // 2
        line = links.gather_line(links.lift(packed))
        order_a, order_b = links.orders()
        first = links.gather_plane(line[..., :half], order_a)
        second = links.gather_plane(line[..., half:], order_b)
        first = links.gather_bit(first, 1).reshape(n * padded, half)
        second = links.gather_bit(second, 1).reshape(n * padded, wide - half)
        out_line = links.gather_line(links.lift(w_output))
        cut = (width // 256) * 128
        out_a = links.gather_bit(links.gather_plane(out_line[..., :cut], order_a), 1)
        out_b = links.gather_bit(links.gather_plane(out_line[..., cut:], order_b), 1)
        output_full = jnp.concatenate([out_a, out_b], axis=-1).reshape(n * out_rows_n, width)

        gate_own = ffn_rows[:, :width]
        up_own = ffn_rows[:, width : 2 * width]
        down_own = ffn_rows[:, 2 * width :]
        gate_full = links.gather_bit(links.gather_plane(links.lift(gate_own), order_a), 1)
        up_full = links.gather_bit(links.gather_plane(links.lift(up_own), order_b), 1)
        down_a = links.gather_bit(
            links.gather_plane(links.lift(down_own[:, :cut]), order_a), 1
        )
        down_b = links.gather_bit(
            links.gather_plane(links.lift(down_own[:, cut:]), order_b), 1
        )
        units = links.dp * ffn_rows.shape[0]
        gate_full = gate_full.reshape(units, width)
        up_full = up_full.reshape(units, width)
        down_full = jnp.concatenate([down_a, down_b], axis=-1).reshape(units, width)

        owners = links.owners()
        gain_blocks = first.reshape(n, padded, half)[:, rows, :gain_n]
        spread_wide = (
            owners[:, None] == (jnp.arange(width, dtype=jnp.int32) // rows)[None, :]
        ).astype(BF16)
        spread_head = (
            owners[:, None] == (jnp.arange(head_size, dtype=jnp.int32) // small)[None, :]
        ).astype(BF16)
        lane = jnp.arange(gain_n, dtype=jnp.int32)[:, None]
        inner_wide = (jnp.arange(width, dtype=jnp.int32) % rows)[None, :]
        inner_head = (jnp.arange(head_size, dtype=jnp.int32) % small)[None, :]
        masks = [lane == inner_wide + k * rows for k in range(4)] + [
            lane == inner_head + 4 * rows + k * small for k in range(2)
        ]
        wide_gains = cross_rows(gain_blocks, spread_wide)
        head_gains = cross_rows(gain_blocks, spread_head)
        g_attn_pre, g_attn_post, g_ffn_pre, g_ffn_post = (
            jnp.sum(jnp.where(masks[k], wide_gains, 0.0), axis=0) for k in range(4)
        )
        g_query, g_key = (
            jnp.sum(jnp.where(masks[4 + k], head_gains, 0.0), axis=0) for k in range(2)
        )

        position, allowed = layout_of(seq_ids)
        cosine, sine = rotary_tables(position, head_size)
        live = (seq_ids >= 0).astype(F32)[:, None]
        inputs = tokens.astype(F32)
        unit_in, factor_in = normalize(inputs)
        attn_in = (unit_in * g_attn_pre).astype(BF16)
        choose_in = one_hot_rows(owners, rows, padded)
        choose_out = one_hot_rows(owners, out_rows_n, out_rows_n)
        attn_sel = product(attn_in, choose_in).astype(BF16)
        projected = jnp.concatenate(
            [product(attn_sel, first), product(attn_sel, second)], axis=1
        )
        queries = projected[:, :q_width].reshape(count, heads, head_size)
        key_rows = projected[:, q_width : q_width + head_size][:, None, :]
        value_rows = projected[:, q_width + head_size :].astype(BF16)
        unit_query, factor_query = normalize(queries)
        unit_key, factor_key = normalize(key_rows)
        query_rot = rotary(unit_query * g_query, cosine, sine).astype(BF16)
        key_rot = rotary(unit_key * g_key, cosine, sine)[:, 0, :].astype(BF16)
        scores = batched("qhd,kd->hqk", query_rot, key_rot) * SCALE
        expo = jnp.where(allowed[None], jnp.exp(scores), 0.0)
        denom = jnp.sum(expo, axis=-1, keepdims=True)
        logsum = jnp.log(denom)
        probs = (expo / denom).astype(BF16)
        mixed = (
            batched("hqk,kd->qhd", probs, value_rows).reshape(count, q_width).astype(BF16)
        )
        mixed_sel = product(mixed, choose_out).astype(BF16)
        attn_raw = product(mixed_sel, output_full)
        unit_post, factor_post = normalize(attn_raw)
        resid = inputs + unit_post * g_attn_post
        unit_ffn, factor_ffn = normalize(resid)
        ffn_in = (unit_ffn * g_ffn_pre).astype(BF16)

        rows_in = [ffn_in] + [links.swap(ffn_in, "fsdp", k) for k in range(1, links.fsdp)]
        saved = []
        ffn_raw = None
        parts = []
        for k in list(range(1, links.fsdp)) + [0]:
            gate = cross_cols(rows_in[k], gate_full)
            up = cross_cols(rows_in[k], up_full)
            gelu_val, gelu_slope = gelu_pair(gate)
            hidden = (gelu_val * up).astype(BF16)
            part = product(hidden, down_full)
            if k:
                part = links.swap(part.astype(BF16), "fsdp", k).astype(F32)
            parts.append(part)
            saved.append((k, gelu_val, up * gelu_slope))
        ffn_raw = sum(parts[1:], parts[0])
        unit_last, factor_last = normalize(ffn_raw)
        out_rows = resid + unit_last * g_ffn_post
        activations = (live * out_rows).astype(BF16)

        cot_live = cotangent.astype(F32) * live
        grad_ffn_post = jnp.sum(cot_live * unit_last, axis=0)
        d_ffn_raw = norm_back(cot_live * g_ffn_post, unit_last, factor_last).astype(BF16)
        rows_back = [d_ffn_raw] + [links.swap(d_ffn_raw, "fsdp", k) for k in range(1, links.fsdp)]
        parts = []
        for k, gelu_val, up_slope in saved:
            d_hidden = cross_cols(rows_back[k], down_full)
            d_gate = (d_hidden * up_slope).astype(BF16)
            d_up = (d_hidden * gelu_val).astype(BF16)
            part = product(d_gate, gate_full) + product(d_up, up_full)
            if k:
                part = links.swap(part.astype(BF16), "fsdp", k).astype(F32)
            parts.append(part)
        d_ffn_in = sum(parts[1:], parts[0])

        def everyone(blocks):
            block = links.lift(jnp.stack(blocks, axis=0))
            block = block.reshape(block.shape[:-4] + block.shape[-3:])
            left = links.gather_bit(links.gather_plane(block[..., :cut], order_a), 1)
            right = links.gather_bit(links.gather_plane(block[..., cut:], order_b), 1)
            return jnp.concatenate([left, right], axis=-1).reshape(n * count, width)

        all_in = everyone(rows_in)
        own_gate = cross_cols(gate_own, all_in)
        own_up = cross_cols(up_own, all_in)
        own_gelu, own_slope = gelu_pair(own_gate)
        own_hidden = (own_gelu * own_up).astype(BF16)
        own_up_slope = own_up * own_slope
        all_back = everyone(rows_back)
        own_d_hidden = cross_cols(down_own, all_back)
        own_d_gate = (own_d_hidden * own_up_slope).astype(BF16)
        own_d_up = (own_d_hidden * own_gelu).astype(BF16)
        grad_ffn = jnp.concatenate(
            [product(own_d_gate, all_in), product(own_d_up, all_in), product(own_hidden, all_back)],
            axis=1,
        )

        grad_ffn_pre = jnp.sum(d_ffn_in * unit_ffn, axis=0)
        d_resid = cot_live + norm_back(d_ffn_in * g_ffn_pre, unit_ffn, factor_ffn)
        grad_attn_post = jnp.sum(d_resid * unit_post, axis=0)
        d_attn_raw = norm_back(d_resid * g_attn_post, unit_post, factor_post).astype(BF16)
        grad_output = cross_rows(mixed_sel, d_attn_raw)
        d_mixed_sel = cross_cols(d_attn_raw, output_full).astype(BF16)
        d_mixed = cross_cols(d_mixed_sel, choose_out).astype(BF16)
        d_heads = d_mixed.reshape(count, heads, head_size)
        probs_back = jnp.where(allowed[None], jnp.exp(scores - logsum), 0.0)
        d_probs = batched("qhd,kd->hqk", d_heads, value_rows)
        row_dot = jnp.sum(probs_back * d_probs, axis=-1, keepdims=True)
        d_scores = (probs_back * (d_probs - row_dot) * SCALE).astype(BF16)
        d_values = batched("hqk,qhd->kd", probs_back.astype(BF16), d_heads).astype(BF16)
        d_query_rot = batched("hqk,kd->qhd", d_scores, key_rot)
        d_key_rot = batched("hqk,qhd->kd", d_scores, query_rot)
        d_unit_query = rotary(d_query_rot, cosine, -sine)
        d_unit_key = rotary(d_key_rot[:, None, :], cosine, -sine)
        grad_qgain = jnp.sum(d_unit_query * unit_query, axis=(0, 1))
        grad_kgain = jnp.sum(d_unit_key * unit_key, axis=(0, 1))
        d_queries = (
            norm_back(d_unit_query * g_query, unit_query, factor_query)
            .reshape(count, q_width)
            .astype(BF16)
        )
        d_keys = norm_back(d_unit_key * g_key, unit_key, factor_key)[:, 0, :].astype(BF16)
        d_projected = jnp.concatenate([d_queries, d_keys, d_values], axis=1)
        d_attn_sel = cross_cols(d_projected[:, :half], first) + cross_cols(
            d_projected[:, half:], second
        )
        high, middle, low = split3(d_attn_sel)
        d_attn_in = (
            cross_cols(high, choose_in) + cross_cols(middle, choose_in) + cross_cols(low, choose_in)
        )
        grad_attn_pre = jnp.sum(d_attn_in * unit_in, axis=0)
        token_grad = d_resid + norm_back(d_attn_in * g_attn_pre, unit_in, factor_in)

        wide_grads = (grad_attn_pre, grad_attn_post, grad_ffn_pre, grad_ffn_post)
        head_grads = (grad_qgain, grad_kgain)
        wide_field = sum(
            jnp.where(masks[k], wide_grads[k].astype(BF16)[None, :], 0) for k in range(4)
        )
        head_field = sum(
            jnp.where(masks[4 + k], head_grads[k].astype(BF16)[None, :], 0) for k in range(2)
        )
        gain_field = cross_cols(spread_wide, wide_field) + cross_cols(spread_head, head_field)

        def owned(value, order):
            value = links.reduce_bit(value, 1)
            for bit in order[::-1]:
                value = links.reduce_bit(value, bit)
            return links.reduce_line(value)

        lead = (2,) * len(links.bits) + (links.fsdp,)
        grad_first = cross_rows(attn_sel, d_projected[:, :half]).reshape(n, padded, half)
        grad_first = grad_first.at[:, rows, :gain_n].set(gain_field)
        grad_second = cross_rows(attn_sel, d_projected[:, half:])
        sum_first = owned(grad_first.reshape(lead + (padded, half)), order_a)
        sum_second = owned(grad_second.reshape(lead + (padded, wide - half)), order_b)
        sum_first = sum_first.reshape(padded, half)
        sum_second = sum_second.reshape(padded, wide - half)
        sum_wide = jnp.concatenate([sum_first[:rows], sum_second[:rows]], axis=1)
        grad_output = grad_output.reshape(lead + (out_rows_n, width))
        sum_out_a = owned(grad_output[..., :cut], order_a).reshape(out_rows_n, cut)
        sum_out_b = owned(grad_output[..., cut:], order_b).reshape(out_rows_n, width - cut)
        sum_out = jnp.concatenate([sum_out_a, sum_out_b], axis=1)
        sums = sum_first[rows]
        return (
            activations,
            token_grad,
            sum_wide[:, :q_width],
            sum_wide[:, q_width : q_width + head_size],
            sum_wide[:, q_width + head_size :],
            sum_out,
            grad_ffn,
            sums[:rows],
            sums[rows : 2 * rows],
            sums[4 * rows : 4 * rows + small],
            sums[4 * rows + small : 4 * rows + 2 * small],
            sums[2 * rows : 3 * rows],
            sums[3 * rows : 4 * rows],
        )

    return local


def solution(mesh):
    both = ("dp", "fsdp")
    matrix = P(both, None)
    vector = P(both)
    return jax.shard_map(
        make_local(mesh),
        mesh=mesh,
        in_specs=(matrix, matrix, vector) + (matrix,) * 5 + (vector,) * 6,
        out_specs=(matrix,) * 7 + (vector,) * 6,
        check_vma=False,
    )
```

time: 1230 us -> 446 us (0.36)
  blocking collectives: 430 us -> 0 us
  waiting for transfers between devices: 564 us -> 176 us
  other arithmetic: 15.1 us -> 59.2 us
  starting transfers between devices: 34.5 us -> 75.2 us
  matrix products: 133 us -> 93 us
  between operations: 15.9 us -> 3.17 us
    all_gather x7 -> x0, waiting for transfers between devices: 554 us -> none  [the longest x1 237 us: local(): piece = lax.all_gather(ffn_rows, ('dp', 'fsdp'), axis=0, tiled=True)]
    unnamed x3 -> x0, blocking collectives: 279 us -> none
    ppermute x0 -> x78, waiting for transfers between devices: none -> 176 us  [swap(): return lax.ppermute(value, axis, [(i, i ^ offset) for i in range(size)])]
    all_gather x2 -> x0, blocking collectives: 150 us -> none  [the longest x1 77.4 us: local(): lax.all_gather(shards[1], ('dp', 'fsdp'), axis=0, tiled=True)]
    ppermute x0 -> x78, starting transfers between devices: none -> 75.2 us  [swap(): return lax.ppermute(value, axis, [(i, i ^ offset) for i in range(size)])]
    unnamed x12 -> x0, starting transfers between devices: 33.6 us -> none
    concatenate x1 -> x38, other arithmetic: 1.81 us -> 31.8 us  [the longest x28 17.8 us: gather_bit(): jnp.concatenate([value, self.swap(value, 'dp', bit)], axis=self.bits.inde...]
    dot_general x7 -> x5, matrix products: 25.1 us -> 6.83 us  [cross_rows(): lax.dot_general(left, right, (((0,), (0,)), ((), ())), preferred_element_...]
  transfers between devices with their start and end apart: 20 -> 78, of which waited for: 7 -> 31; matrix products, arithmetic and copies ran while one was open for 26% -> 35% of each run, Pallas kernels for 0% -> 0%
where the time goes in v1:
time: 446 us; the launch traced here: 439 us
  waiting for transfers between devices  176 us (39%)
  matrix products  93 us (21%)
  starting transfers between devices  75.2 us (17%)
  other arithmetic  59.2 us (13%)
  local copies, waits for them, and re-layouts  32.6 us (7%)
    ppermute x78, waiting for transfers between devices, swap(): return lax.ppermute(value, axis, [(i, i ^ offset) for i in range(size)])  176 us
    ppermute x78, starting transfers between devices, swap(): return lax.ppermute(value, axis, [(i, i ^ offset) for i in range(size)])  75.2 us
    dot_general x23, matrix products, cross_cols(): lax.dot_general(left, right, (((1,), (1,)), ((), ())), preferred_element_...  49.4 us
    dot_general x20, matrix products, product(): return jnp.dot(left, right, preferred_element_type=F32)  27.8 us
    concatenate x28, other arithmetic, gather_bit(): jnp.concatenate([value, self.swap(value, 'dp', bit)], axis=self.bits.inde...  17.8 us
    dot_general x6, matrix products, batched(): return jnp.einsum(form, left, right, preferred_element_type=F32)  8.95 us
  transfers between devices with their start and end apart: 78, of which 31 were waited for; matrix products, arithmetic and copies ran while one was open for 35% of the time, Pallas kernels for 0%

profile of v1, /device:TPU:4, one launch (start us, length us, event | category | flops | bytes accessed | tf_op | source)
XLA Modules:
  0.0 438.9 jit_solution(7952148223436023117)
XLA Ops:
  0.7 4.1 concatenate.176
  5.8 3.7 collective-permute-start.2
  31.0 16.0 %collective-permute-done.12 = bf16[1,1,1,4,32,512]{5,4,3,2,1,0:T(8,128)(2,1)S(1)} collective-permute-done((bf16[1,1,1,4,32,512]{5,4,3,2,1,0:T(8,128)(2,1)S(1)}, bf16[1,1,1,4,32,512]{5,4,3,2,1,0:T(8,128)(2,1)S(1)}, u32[]{:S(2)}, u32[]{:S(2)}) %collective-permute-start.12) | collective-permute-done | bytes 131104 | tf_op jit(solution)/shard_map/ppermute | solution.py:90
  48.3 4.9 %collective-permute-done.15 = bf16[1,1,1,4,32,640]{5,4,3,2,1,0:T(8,128)(2,1)S(1)} collective-permute-done((bf16[1,1,1,4,32,640]{5,4,3,2,1,0:T(8,128)(2,1)S(1)}, bf16[1,1,1,4,32,640]{5,4,3,2,1,0:T(8,128)(2,1)S(1)}, u32[]{:S(2)}, u32[]{:S(2)}) %collective-permute-start.15) | collective-permute-done | bytes 163872 | tf_op jit(solution)/shard_map/ppermute | solution.py:90
  56.1 5.9 %collective-permute-done.6 = bf16[1,1,1,4,40,768]{5,4,3,2,1,0:T(8,128)(2,1)S(1)} collective-permute-done((bf16[1,1,1,4,40,768]{5,4,3,2,1,0:T(8,128)(2,1)S(1)}, bf16[1,1,1,4,40,768]{5,4,3,2,1,0:T(8,128)(2,1)S(1)}, u32[]{:S(2)}, u32[]{:S(2)}) %collective-permute-start.6) | collective-permute-done | bytes 245792 | tf_op jit(solution)/shard_map/ppermute | solution.py:90
  62.6 5.1 %collective-permute-done.13 = bf16[1,2,1,4,32,512]{5,4,3,2,1,0:T(8,128)(2,1)S(1)} collective-permute-done((bf16[1,2,1,4,32,512]{5,4,3,2,1,0:T(8,128)(2,1)S(1)}, bf16[1,2,1,4,32,512]{5,4,3,2,1,0:T(8,128)(2,1)S(1)}, u32[]{:S(2)}, u32[]{:S(2)}) %collective-permute-start.13) | collective-permute-done | bytes 262176 | tf_op jit(solution)/shard_map/ppermute | solution.py:90
  68.8 3.8 collective-permute-done.16
  73.4 3.7 collective-permute-done.26
  78.2 4.6 %collective-permute-done.29 = bf16[1,1,2,1,216,640]{5,4,3,2,1,0:T(8,128)(2,1)S(1)} collective-permute-done((bf16[1,1,2,1,216,640]{5,4,3,2,1,0:T(8,128)(2,1)S(1)}, bf16[1,1,2,1,216,640]{5,4,3,2,1,0:T(8,128)(2,1)S(1)}, u32[]{:S(2)}, u32[]{:S(2)}) %collective-permute-start.29) | collective-permute-done | bytes 552992 | tf_op jit(solution)/shard_map/ppermute | solution.py:90
  85.9 7.5 %collective-permute-done.7 = bf16[1,1,2,4,40,768]{5,4,3,2,1,0:T(8,128)(2,1)S(1)} collective-permute-done((bf16[1,1,2,4,40,768]{5,4,3,2,1,0:T(8,128)(2,1)S(1)}, bf16[1,1,2,4,40,768]{5,4,3,2,1,0:T(8,128)(2,1)S(1)}, u32[]{:S(2)}, u32[]{:S(2)}) %collective-permute-start.7) | collective-permute-done | bytes 491552 | tf_op jit(solution)/shard_map/ppermute | solution.py:90
  96.2 12.5 %collective-permute-done.23 = bf16[1,1,2,1,216,1152]{5,4,3,2,1,0:T(8,128)(2,1)S(1)} collective-permute-done((bf16[1,1,2,1,216,1152]{5,4,3,2,1,0:T(8,128)(2,1)S(1)}, bf16[1,1,2,1,216,1152]{5,4,3,2,1,0:T(8,128)(2,1)S(1)}, u32[]{:S(2)}, u32[]{:S(2)}) %collective-permute-start.23) | collective-permute-done | bytes 995360 | tf_op jit(solution)/shard_map/ppermute | solution.py:90
  142.2 14.5 %collective-permute-done.32 = bf16[128,1152]{1,0:T(8,128)(2,1)} collective-permute-done((bf16[128,1152]{1,0:T(8,128)(2,1)}, bf16[128,1152]{1,0:T(8,128)(2,1)}, u32[]{:S(2)}, u32[]{:S(2)}) %collective-permute-start.32) | collective-permute-done | bytes 294944 | tf_op jit(solution)/shard_map/ppermute | solution.py:90
  162.2 10.7 %collective-permute-done.72 = bf16[1,1,1,4,128,512]{5,4,3,2,1,0:T(8,128)(2,1)S(1)} collective-permute-done((bf16[1,1,1,4,128,512]{5,4,3,2,1,0:T(8,128)(2,1)S(1)}, bf16[1,1,1,4,128,512]{5,4,3,2,1,0:T(8,128)(2,1)S(1)}, u32[]{:S(2)}, u32[]{:S(2)}) %collective-permute-start.72) | collective-permute-done | bytes 524320 | tf_op jit(solution)/shard_map/ppermute | solution.py:90
  195.7 3.4 collective-permute-start.31
  205.1 3.8 collective-permute-done.33
  217.1 2.9 collective-permute-start.36
  221.0 6.4 %collective-permute-done.40 = bf16[128,1152]{1,0:T(8,128)(2,1)S(1)} collective-permute-done((bf16[128,1152]{1,0:T(8,128)(2,1)S(1)}, bf16[128,1152]{1,0:T(8,128)(2,1)S(1)}, u32[]{:S(2)}, u32[]{:S(2)}) %collective-permute-start.40) | collective-permute-done | bytes 294944 | tf_op jit(solution)/shard_map/ppermute | solution.py:90
  232.4 20.7 %collective-permute-done.38 = bf16[128,1152]{1,0:T(8,128)(2,1)S(1)} collective-permute-done((bf16[128,1152]{1,0:T(8,128)(2,1)S(1)}, bf16[128,1152]{1,0:T(8,128)(2,1)S(1)}, u32[]{:S(2)}, u32[]{:S(2)}) %collective-permute-start.38) | collective-permute-done | bytes 294944 | tf_op jit(solution)/shard_map/ppermute | solution.py:90
  272.6 4.2 fusion.32
  297.2 3.1 fusion.153
  325.3 2.8 collective-permute-start.59
  336.7 23.6 %collective-permute-done.62 = bf16[1,1,1,4,32,640]{5,4,3,2,1,0:T(8,128)(2,1)S(1)} collective-permute-done((bf16[1,1,1,4,32,640]{5,4,3,2,1,0:T(8,128)(2,1)S(1)}, bf16[1,1,1,4,32,640]{5,4,3,2,1,0:T(8,128)(2,1)S(1)}, u32[]{:S(2)}, u32[]{:S(2)}) %collective-permute-start.62) | collective-permute-done | bytes 163872 | tf_op jit(solution)/shard_map/ppermute | solution.py:90
  360.4 2.8 collective-permute-start.65
  372.4 8.7 %collective-permute-done.43 = bf16[1,2,1,4,40,768]{5,4,3,2,1,0:T(8,128)(2,1)S(1)} collective-permute-done((bf16[1,2,1,4,40,768]{5,4,3,2,1,0:T(8,128)(2,1)S(1)}, bf16[1,2,1,4,40,768]{5,4,3,2,1,0:T(8,128)(2,1)S(1)}, u32[]{:S(2)}, u32[]{:S(2)}) %collective-permute-start.43) | collective-permute-done | bytes 491552 | tf_op jit(solution)/shard_map/ppermute | solution.py:90
  396.5 3.7 collective-permute-start.51
  406.7 5.1 %convolution_bitcast_fusion.1 = f32[216,4096]{1,0:T(8,128)} fusion(bf16[4096,1152]{1,0:T(8,128)(2,1)S(1)} %bitcast.227, bf16[216,3456]{1,0:T(8,128)(2,1)S(1)} %copy-done.54), kind=kOutput, calls=%fused_computation.11 | convolution fusion | flops 2038431744 | bytes 13473792 | tf_op jit(solution)/shard_map/dot_general | solution.py:71
  411.7 5.1 %convolution_bitcast_fusion = f32[216,4096]{1,0:T(8,128)} fusion(bf16[4096,1152]{1,0:T(8,128)(2,1)S(1)} %bitcast.228, bf16[216,3456]{1,0:T(8,128)(2,1)S(1)} %copy-done.54), kind=kOutput, calls=%fused_computation.10 | convolution fusion | flops 2038431744 | bytes 13473792 | tf_op jit(solution)/shard_map/dot_general | solution.py:71
  416.8 5.0 %maximum_maximum_fusion = bf16[2,2,2,4,128,1152]{5,4,3,2,1,0:T(8,128)(2,1)S(1)} fusion(bf16[1,2,2,4,128,640]{5,4,3,2,1,0:T(8,128)(2,1)S(1)} %collective-permute-done.71, bf16[1,1,2,4,128,640]{5,4,3,2,1,0:T(8,128)(2,1)S(1)} %collective-permute-done.70, bf16[1,1,1,4,128,640]{5,4,3,2,1,0:T(8,128)(2,1)} %collective-permute-done.69, ...), kind=kLoop, calls=%fused_computation.1 | loop fusion | flops 75497472 | bytes 18874368 | tf_op jit(solution)/shard_map/concatenate | solution.py:313
  421.8 5.1 %convolution_bitcast_fusion.2 = f32[216,4096]{1,0:T(8,128)} fusion(bf16[4096,1152]{1,0:T(8,128)(2,1)S(1)} %bitcast.231, bf16[216,3456]{1,0:T(8,128)(2,1)S(1)} %copy-done.54), kind=kOutput, calls=%fused_computation.12 | convolution fusion | flops 2038431744 | bytes 13473792 | tf_op jit(solution)/shard_map/dot_general | solution.py:71
  426.9 3.0 fusion.28
  429.9 3.0 fusion.27
  432.8 4.1 fusion.29
  (572 shorter events, 222.4 us)
Async XLA Ops:
  5.8 22.5 %collective-permute-start.2 = (bf16[1,1,1,1,40,1536]{5,4,3,2,1,0:T(8,128)(2,1)S(1)}, bf16[1,1,1,1,40,1536]{5,4,3,2,1,0:T(8,128)(2,1)S(1)}, u32[]{:S(2)}, u32[]{:S(2)}) collective-permute-start(bf16[1,1,1,1,40,1536]{5,4,3,2,1,0:T(8,128)(2,1)S(1)} %fusion.165), channel_id=1, source_target_pairs={{0,3},{1,2},{2,1},{3,0},{4,7},{5,6},{6,5},{7,4},{8,11},{9,10},{10,... | collective-permute-start | bytes 368648 | tf_op jit(solution)/shard_map/ppermute | solution.py:90
  9.4 19.4 %collective-permute-start.1 = (bf16[1,1,1,1,40,1536]{5,4,3,2,1,0:T(8,128)(2,1)S(1)}, bf16[1,1,1,1,40,1536]{5,4,3,2,1,0:T(8,128)(2,1)S(1)}, u32[]{:S(2)}, u32[]{:S(2)}) collective-permute-start(bf16[1,1,1,1,40,1536]{5,4,3,2,1,0:T(8,128)(2,1)S(1)} %fusion.165), channel_id=1, source_target_pairs={{0,2},{1,3},{2,0},{3,1},{4,6},{5,7},{6,4},{7,5},{8,10},{9,11},{10,... | collective-permute-start | bytes 368648 | tf_op jit(solution)/shard_map/ppermute | solution.py:90
  26.2 27.6 %collective-permute-start.28 = (bf16[1,1,1,1,216,640]{5,4,3,2,1,0:T(8,128)(2,1)S(1)}, bf16[1,1,1,1,216,640]{5,4,3,2,1,0:T(8,128)(2,1)S(1)}, u32[]{:S(2)}, u32[]{:S(2)}) collective-permute-start(bf16[1,1,1,1,216,640]{5,4,3,2,1,0:T(8,128)(2,1)S(1)} %slice_bitcast_fusion.2), channel_id=1, source_target_pairs={{0,8},{4,12},{8,0},{12,4},{16,24},{20,28},{24,16},{28,20},{1,9},{5... | collective-permute-start | bytes 829448 | tf_op jit(solution)/shard_map/ppermute | solution.py:90
  27.7 19.9 %collective-permute-start.25 = (bf16[1,1,1,1,216,512]{5,4,3,2,1,0:T(8,128)(2,1)S(1)}, bf16[1,1,1,1,216,512]{5,4,3,2,1,0:T(8,128)(2,1)S(1)}, u32[]{:S(2)}, u32[]{:S(2)}) collective-permute-start(bf16[1,1,1,1,216,512]{5,4,3,2,1,0:T(8,128)(2,1)S(1)} %slice_bitcast_fusion.3), channel_id=1, source_target_pairs={{0,16},{4,20},{8,24},{12,28},{16,0},{20,4},{24,8},{28,12},{1,17},{... | collective-permute-start | bytes 663560 | tf_op jit(solution)/shard_map/ppermute | solution.py:90
  28.3 40.0 %collective-permute-start.22 = (bf16[1,1,1,1,216,1152]{5,4,3,2,1,0:T(8,128)(2,1)S(1)}, bf16[1,1,1,1,216,1152]{5,4,3,2,1,0:T(8,128)(2,1)S(1)}, u32[]{:S(2)}, u32[]{:S(2)}) collective-permute-start(bf16[1,1,1,1,216,1152]{5,4,3,2,1,0:T(8,128)(2,1)S(1)} %get-tuple-element.57), channel_id=1, source_target_pairs={{0,8},{4,12},{8,0},{12,4},{16,24},{20,28},{24,16},{28,20},{1,9},{5... | collective-permute-start | bytes 1493000 | tf_op jit(solution)/shard_map/ppermute | solution.py:90
  28.9 44.4 %collective-permute-start.19 = (bf16[1,1,1,1,216,1152]{5,4,3,2,1,0:T(8,128)(2,1)S(1)}, bf16[1,1,1,1,216,1152]{5,4,3,2,1,0:T(8,128)(2,1)S(1)}, u32[]{:S(2)}, u32[]{:S(2)}) collective-permute-start(bf16[1,1,1,1,216,1152]{5,4,3,2,1,0:T(8,128)(2,1)S(1)} %get-tuple-element.56), channel_id=1, source_target_pairs={{0,16},{4,20},{8,24},{12,28},{16,0},{20,4},{24,8},{28,12},{1,17},{... | collective-permute-start | bytes 1493000 | tf_op jit(solution)/shard_map/ppermute | solution.py:90
  55.5 21.7 %collective-permute-start.26 = (bf16[1,2,1,1,216,512]{5,4,3,2,1,0:T(8,128)(2,1)S(1)}, bf16[1,2,1,1,216,512]{5,4,3,2,1,0:T(8,128)(2,1)S(1)}, u32[]{:S(2)}, u32[]{:S(2)}) collective-permute-start(bf16[1,2,1,1,216,512]{5,4,3,2,1,0:T(8,128)(2,1)S(1)} %pad_maximum_fusion.29), channel_id=1, source_target_pairs={{0,8},{4,12},{8,0},{12,4},{16,24},{20,28},{24,16},{28,20},{1,9},{5... | collective-permute-start | bytes 1327112 | tf_op jit(solution)/shard_map/ppermute | solution.py:90
  72.6 20.7 %collective-permute-start.7 = (bf16[1,1,2,4,40,768]{5,4,3,2,1,0:T(8,128)(2,1)S(1)}, bf16[1,1,2,4,40,768]{5,4,3,2,1,0:T(8,128)(2,1)S(1)}, u32[]{:S(2)}, u32[]{:S(2)}) collective-permute-start(bf16[1,1,2,4,40,768]{5,4,3,2,1,0:T(8,128)(2,1)S(1)} %pad_maximum_fusion.28), channel_id=1, source_target_pairs={{0,16},{4,20},{8,24},{12,28},{16,0},{20,4},{24,8},{28,12},{1,17},{... | collective-permute-start | bytes 1474568 | tf_op jit(solution)/shard_map/ppermute | solution.py:90
  73.3 20.8 %collective-permute-start.17 = (bf16[1,2,2,4,32,640]{5,4,3,2,1,0:T(8,128)(2,1)S(1)}, bf16[1,2,2,4,32,640]{5,4,3,2,1,0:T(8,128)(2,1)S(1)}, u32[]{:S(2)}, u32[]{:S(2)}) collective-permute-start(bf16[1,2,2,4,32,640]{5,4,3,2,1,0:T(8,128)(2,1)S(1)} %pad_maximum_fusion.21), channel_id=1, source_target_pairs={{0,4},{4,0},{8,12},{12,8},{16,20},{20,16},{24,28},{28,24},{1,5},{5... | collective-permute-start | bytes 1966088 | tf_op jit(solution)/shard_map/ppermute | solution.py:90
  82.8 25.8 %collective-permute-start.23 = (bf16[1,1,2,1,216,1152]{5,4,3,2,1,0:T(8,128)(2,1)S(1)}, bf16[1,1,2,1,216,1152]{5,4,3,2,1,0:T(8,128)(2,1)S(1)}, u32[]{:S(2)}, u32[]{:S(2)}) collective-permute-start(bf16[1,1,2,1,216,1152]{5,4,3,2,1,0:T(8,128)(2,1)S(1)} %pad_maximum_fusion.17), channel_id=1, source_target_pairs={{0,16},{4,20},{8,24},{12,28},{16,0},{20,4},{24,8},{28,12},{1,17},{... | collective-permute-start | bytes 2985992 | tf_op jit(solution)/shard_map/ppermute | solution.py:90
  84.5 25.8 %collective-permute-start.20 = (bf16[1,2,1,1,216,1152]{5,4,3,2,1,0:T(8,128)(2,1)S(1)}, bf16[1,2,1,1,216,1152]{5,4,3,2,1,0:T(8,128)(2,1)S(1)}, u32[]{:S(2)}, u32[]{:S(2)}) collective-permute-start(bf16[1,2,1,1,216,1152]{5,4,3,2,1,0:T(8,128)(2,1)S(1)} %pad_maximum_fusion.16), channel_id=1, source_target_pairs={{0,8},{4,12},{8,0},{12,4},{16,24},{20,28},{24,16},{28,20},{1,9},{5... | collective-permute-start | bytes 2985992 | tf_op jit(solution)/shard_map/ppermute | solution.py:90
  93.4 65.4 %collective-permute-start.27 = (bf16[1,2,2,1,216,512]{5,4,3,2,1,0:T(8,128)(2,1)}, bf16[1,2,2,1,216,512]{5,4,3,2,1,0:T(8,128)(2,1)}, u32[]{:S(2)}, u32[]{:S(2)}) collective-permute-start(bf16[1,2,2,1,216,512]{5,4,3,2,1,0:T(8,128)(2,1)} %pad_maximum_fusion.20), channel_id=1, source_target_pairs={{0,4},{4,0},{8,12},{12,8},{16,20},{20,16},{24,28},{28,24},{1,5},{5... | collective-permute-start | bytes 2654216 | tf_op jit(solution)/shard_map/ppermute | solution.py:90
  93.5 66.1 %collective-permute-start.30 = (bf16[1,2,2,1,216,640]{5,4,3,2,1,0:T(8,128)(2,1)}, bf16[1,2,2,1,216,640]{5,4,3,2,1,0:T(8,128)(2,1)}, u32[]{:S(2)}, u32[]{:S(2)}) collective-permute-start(bf16[1,2,2,1,216,640]{5,4,3,2,1,0:T(8,128)(2,1)} %pad_maximum_fusion.13), channel_id=1, source_target_pairs={{0,4},{4,0},{8,12},{12,8},{16,20},{20,16},{24,28},{28,24},{1,5},{5... | collective-permute-start | bytes 3317768 | tf_op jit(solution)/shard_map/ppermute | solution.py:90
  130.8 25.8 %collective-permute-start.32 = (bf16[128,1152]{1,0:T(8,128)(2,1)}, bf16[128,1152]{1,0:T(8,128)(2,1)}, u32[]{:S(2)}, u32[]{:S(2)}) collective-permute-start(bf16[128,1152]{1,0:T(8,128)(2,1)} %multiply_convert_fusion.15), channel_id=1, source_target_pairs={{0,2},{1,3},{2,0},{3,1},{4,6},{5,7},{6,4},{7,5},{8,10},{9,11},{10,... | collective-permute-start | bytes 884744 | tf_op jit(solution)/shard_map/ppermute | solution.py:90
  130.8 25.8 %collective-permute-start.18 = (bf16[128,1152]{1,0:T(8,128)(2,1)}, bf16[128,1152]{1,0:T(8,128)(2,1)}, u32[]{:S(2)}, u32[]{:S(2)}) collective-permute-start(bf16[128,1152]{1,0:T(8,128)(2,1)} %multiply_convert_fusion.15), channel_id=1, source_target_pairs={{0,1},{1,0},{2,3},{3,2},{4,5},{5,4},{6,7},{7,6},{8,9},{9,8},{10,11... | collective-permute-start | bytes 884744 | tf_op jit(solution)/shard_map/ppermute | solution.py:90
  140.9 35.4 %collective-permute-start.24 = (bf16[1,2,2,1,216,1152]{5,4,3,2,1,0:T(8,128)(2,1)}, bf16[1,2,2,1,216,1152]{5,4,3,2,1,0:T(8,128)(2,1)S(1)}, u32[]{:S(2)}, u32[]{:S(2)}) collective-permute-start(bf16[1,2,2,1,216,1152]{5,4,3,2,1,0:T(8,128)(2,1)} %pad_maximum_fusion.8), channel_id=1, source_target_pairs={{0,4},{4,0},{8,12},{12,8},{16,20},{20,16},{24,28},{28,24},{1,5},{5... | collective-permute-start | bytes 5971976 | tf_op jit(solution)/shard_map/ppermute | solution.py:90
  156.6 20.5 %collective-permute-start.21 = (bf16[1,2,2,1,216,1152]{5,4,3,2,1,0:T(8,128)(2,1)}, bf16[1,2,2,1,216,1152]{5,4,3,2,1,0:T(8,128)(2,1)S(1)}, u32[]{:S(2)}, u32[]{:S(2)}) collective-permute-start(bf16[1,2,2,1,216,1152]{5,4,3,2,1,0:T(8,128)(2,1)} %pad_maximum_fusion.7), channel_id=1, source_target_pairs={{0,4},{4,0},{8,12},{12,8},{16,20},{20,16},{24,28},{28,24},{1,5},{5... | collective-permute-start | bytes 5971976 | tf_op jit(solution)/shard_map/ppermute | solution.py:90
  173.0 30.5 %collective-permute-start.73 = (bf16[1,2,1,4,128,512]{5,4,3,2,1,0:T(8,128)(2,1)S(1)}, bf16[1,2,1,4,128,512]{5,4,3,2,1,0:T(8,128)(2,1)S(1)}, u32[]{:S(2)}, u32[]{:S(2)}) collective-permute-start(bf16[1,2,1,4,128,512]{5,4,3,2,1,0:T(8,128)(2,1)S(1)} %pad_maximum_fusion.15), channel_id=1, source_target_pairs={{0,8},{4,12},{8,0},{12,4},{16,24},{20,28},{24,16},{28,20},{1,9},{5... | collective-permute-start | bytes 3145736 | tf_op jit(solution)/shard_map/ppermute | solution.py:90
  176.0 87.7 %collective-permute-start.76 = (bf16[1,1,2,4,128,640]{5,4,3,2,1,0:T(8,128)(2,1)S(1)}, bf16[1,1,2,4,128,640]{5,4,3,2,1,0:T(8,128)(2,1)S(1)}, u32[]{:S(2)}, u32[]{:S(2)}) collective-permute-start(bf16[1,1,2,4,128,640]{5,4,3,2,1,0:T(8,128)(2,1)S(1)} %pad_maximum_fusion.12), channel_id=1, source_target_pairs={{0,16},{4,20},{8,24},{12,28},{16,0},{20,4},{24,8},{28,12},{1,17},{... | collective-permute-start | bytes 3932168 | tf_op jit(solution)/shard_map/ppermute | solution.py:90
  183.9 21.3 %collective-permute-start.35 = (bf16[128,1152]{1,0:T(8,128)(2,1)S(1)}, bf16[128,1152]{1,0:T(8,128)(2,1)S(1)}, u32[]{:S(2)}, u32[]{:S(2)}) collective-permute-start(bf16[128,1152]{1,0:T(8,128)(2,1)S(1)} %convolution_convert_fusion), channel_id=1, source_target_pairs={{0,3},{1,2},{2,1},{3,0},{4,7},{5,6},{6,5},{7,4},{8,11},{9,10},{10,... | collective-permute-start | bytes 884744 | tf_op jit(solution)/shard_map/ppermute | solution.py:90
  217.1 36.0 %collective-permute-start.38 = (bf16[128,1152]{1,0:T(8,128)(2,1)S(1)}, bf16[128,1152]{1,0:T(8,128)(2,1)S(1)}, u32[]{:S(2)}, u32[]{:S(2)}) collective-permute-start(bf16[128,1152]{1,0:T(8,128)(2,1)S(1)} %get-tuple-element.62), channel_id=1, source_target_pairs={{0,2},{1,3},{2,0},{3,1},{4,6},{5,7},{6,4},{7,5},{8,10},{9,11},{10,... | collective-permute-start | bytes 884744 | tf_op jit(solution)/shard_map/ppermute | solution.py:90
  217.1 39.5 %collective-permute-start.36 = (bf16[128,1152]{1,0:T(8,128)(2,1)S(1)}, bf16[128,1152]{1,0:T(8,128)(2,1)S(1)}, u32[]{:S(2)}, u32[]{:S(2)}) collective-permute-start(bf16[128,1152]{1,0:T(8,128)(2,1)S(1)} %get-tuple-element.62), channel_id=1, source_target_pairs={{0,1},{1,0},{2,3},{3,2},{4,5},{5,4},{6,7},{7,6},{8,9},{9,8},{10,11... | collective-permute-start | bytes 884744 | tf_op jit(solution)/shard_map/ppermute | solution.py:90
  230.9 35.7 %collective-permute-start.41 = (bf16[128,1152]{1,0:T(8,128)(2,1)S(1)}, bf16[128,1152]{1,0:T(8,128)(2,1)S(1)}, u32[]{:S(2)}, u32[]{:S(2)}) collective-permute-start(bf16[128,1152]{1,0:T(8,128)(2,1)S(1)} %fusion.23), channel_id=1, source_target_pairs={{0,3},{1,2},{2,1},{3,0},{4,7},{5,6},{6,5},{7,4},{8,11},{9,10},{10,... | collective-permute-start | bytes 884744 | tf_op jit(solution)/shard_map/ppermute | solution.py:90
  263.0 65.1 %collective-permute-start.69 = (bf16[1,1,1,4,128,640]{5,4,3,2,1,0:T(8,128)(2,1)}, bf16[1,1,1,4,128,640]{5,4,3,2,1,0:T(8,128)(2,1)}, u32[]{:S(2)}, u32[]{:S(2)}) collective-permute-start(bf16[1,1,1,4,128,640]{5,4,3,2,1,0:T(8,128)(2,1)} %slice.485), channel_id=1, source_target_pairs={{0,8},{4,12},{8,0},{12,4},{16,24},{20,28},{24,16},{28,20},{1,9},{5... | collective-permute-start | bytes 1966088 | tf_op jit(solution)/shard_map/ppermute | solution.py:90
  263.7 54.6 %collective-permute-start.66 = (bf16[1,1,1,4,128,512]{5,4,3,2,1,0:T(8,128)(2,1)}, bf16[1,1,1,4,128,512]{5,4,3,2,1,0:T(8,128)(2,1)}, u32[]{:S(2)}, u32[]{:S(2)}) collective-permute-start(bf16[1,1,1,4,128,512]{5,4,3,2,1,0:T(8,128)(2,1)} %slice.484), channel_id=1, source_target_pairs={{0,16},{4,20},{8,24},{12,28},{16,0},{20,4},{24,8},{28,12},{1,17},{... | collective-permute-start | bytes 1572872 | tf_op jit(solution)/shard_map/ppermute | solution.py:90
  304.4 32.0 %collective-permute-start.48 = (bf16[1,2,2,4,40,768]{5,4,3,2,1,0:T(8,128)(2,1)S(1)}, bf16[1,2,2,4,40,768]{5,4,3,2,1,0:T(8,128)(2,1)S(1)}, u32[]{:S(2)}, u32[]{:S(2)}) collective-permute-start(bf16[1,2,2,4,40,768]{5,4,3,2,1,0:T(8,128)(2,1)S(1)} %bitcast.245), channel_id=1, source_target_pairs={{0,4},{4,0},{8,12},{12,8},{16,20},{20,16},{24,28},{28,24},{1,5},{5... | collective-permute-start | bytes 2949128 | tf_op jit(solution)/shard_map/ppermute | solution.py:90
  331.1 32.1 %collective-permute-start.42 = (bf16[1,2,2,4,40,768]{5,4,3,2,1,0:T(8,128)(2,1)S(1)}, bf16[1,2,2,4,40,768]{5,4,3,2,1,0:T(8,128)(2,1)S(1)}, u32[]{:S(2)}, u32[]{:S(2)}) collective-permute-start(bf16[1,2,2,4,40,768]{5,4,3,2,1,0:T(8,128)(2,1)S(1)} %bitcast.246), channel_id=1, source_target_pairs={{0,4},{4,0},{8,12},{12,8},{16,20},{20,16},{24,28},{28,24},{1,5},{5... | collective-permute-start | bytes 2949128 | tf_op jit(solution)/shard_map/ppermute | solution.py:90
  332.9 38.0 %collective-permute-start.67 = (bf16[1,2,1,4,128,512]{5,4,3,2,1,0:T(8,128)(2,1)S(1)}, bf16[1,2,1,4,128,512]{5,4,3,2,1,0:T(8,128)(2,1)S(1)}, u32[]{:S(2)}, u32[]{:S(2)}) collective-permute-start(bf16[1,2,1,4,128,512]{5,4,3,2,1,0:T(8,128)(2,1)S(1)} %pad_maximum_fusion.14), channel_id=1, source_target_pairs={{0,8},{4,12},{8,0},{12,4},{16,24},{20,28},{24,16},{28,20},{1,9},{5... | collective-permute-start | bytes 3145736 | tf_op jit(solution)/shard_map/ppermute | solution.py:90
  334.5 49.3 %collective-permute-start.70 = (bf16[1,1,2,4,128,640]{5,4,3,2,1,0:T(8,128)(2,1)S(1)}, bf16[1,1,2,4,128,640]{5,4,3,2,1,0:T(8,128)(2,1)S(1)}, u32[]{:S(2)}, u32[]{:S(2)}) collective-permute-start(bf16[1,1,2,4,128,640]{5,4,3,2,1,0:T(8,128)(2,1)S(1)} %pad_maximum_fusion.11), channel_id=1, source_target_pairs={{0,16},{4,20},{8,24},{12,28},{16,0},{20,4},{24,8},{28,12},{1,17},{... | collective-permute-start | bytes 3932168 | tf_op jit(solution)/shard_map/ppermute | solution.py:90
  335.2 25.1 %collective-permute-start.62 = (bf16[1,1,1,4,32,640]{5,4,3,2,1,0:T(8,128)(2,1)S(1)}, bf16[1,1,1,4,32,640]{5,4,3,2,1,0:T(8,128)(2,1)S(1)}, u32[]{:S(2)}, u32[]{:S(2)}) collective-permute-start(bf16[1,1,1,4,32,640]{5,4,3,2,1,0:T(8,128)(2,1)S(1)} %slice.603), channel_id=1, source_target_pairs={{0,8},{4,12},{8,0},{12,4},{16,24},{20,28},{24,16},{28,20},{1,9},{5... | collective-permute-start | bytes 491528 | tf_op jit(solution)/shard_map/ppermute | solution.py:90
  366.3 38.9 %collective-permute-start.74 = (bf16[1,2,2,4,128,512]{5,4,3,2,1,0:T(8,128)(2,1)S(1)}, bf16[1,2,2,4,128,512]{5,4,3,2,1,0:T(8,128)(2,1)S(1)}, u32[]{:S(2)}, u32[]{:S(2)}) collective-permute-start(bf16[1,2,2,4,128,512]{5,4,3,2,1,0:T(8,128)(2,1)S(1)} %copy-done.48), channel_id=1, source_target_pairs={{0,4},{4,0},{8,12},{12,8},{16,20},{20,16},{24,28},{28,24},{1,5},{5... | collective-permute-start | bytes 6291464 | tf_op jit(solution)/shard_map/ppermute | solution.py:90
  370.9 34.3 %collective-permute-start.77 = (bf16[1,2,2,4,128,640]{5,4,3,2,1,0:T(8,128)(2,1)S(1)}, bf16[1,2,2,4,128,640]{5,4,3,2,1,0:T(8,128)(2,1)S(1)}, u32[]{:S(2)}, u32[]{:S(2)}) collective-permute-start(bf16[1,2,2,4,128,640]{5,4,3,2,1,0:T(8,128)(2,1)S(1)} %copy-done.43), channel_id=1, source_target_pairs={{0,4},{4,0},{8,12},{12,8},{16,20},{20,16},{24,28},{28,24},{1,5},{5... | collective-permute-start | bytes 7864328 | tf_op jit(solution)/shard_map/ppermute | solution.py:90
  (163 other events, 2729.1 us)
